TPU v7x, 256 devices: a whole 4x4x8 slice. The times are simulated.
256 devices in a mesh: expert: 8 (over y_lo, x), fsdp: 32 (over y_hi, z, core).
Axes of the slice: x: 4, y: 4 (y_hi: 2, y_lo: 2; y = y_hi * 2 + y_lo), z: 8, core: 2. Of those that a mesh axis runs over, the one named last changes fastest.
Arguments:
- tokens: bfloat16 [1024, 3072], P('expert'), may hold values from -6 to 6
- assignment: int32 [1024, 2], P('expert'), may hold values from 0 to 7, all different within a row; in each aligned block of 128 rows (0 to 127, 128 to 255, ...) at most 48 rows name the same one
- route_weight: float32 [1024, 2], P('expert'), may hold values from 0.25 to 1
- cotangent: bfloat16 [1024, 3072], P('expert'), may hold values from -6 to 6
- w_gate: bfloat16 [8, 3072, 8192], P('expert', None, 'fsdp'), may hold values from -0.109375 to 0.109375
- w_up: bfloat16 [8, 3072, 8192], P('expert', None, 'fsdp'), may hold values from -0.109375 to 0.109375
- w_down: bfloat16 [8, 8192, 3072], P('expert', 'fsdp'), may hold values from -0.0625 to 0.0625
Outputs:
- moe_out: bfloat16 [1024, 3072], P('expert')
- grad_tokens: bfloat16 [1024, 3072], P('expert')
- grad_prob: float32 [1024, 2], P('expert')
- grad_gate: bfloat16 [8, 3072, 8192], P('expert', None, 'fsdp')
- grad_up: bfloat16 [8, 3072, 8192], P('expert', None, 'fsdp')
- grad_down: bfloat16 [8, 8192, 3072], P('expert', 'fsdp')
Inputs may be any that keep to these rules, and one draw needn't show every extreme that they name: `assignment`: each token names two different experts. Among the 128 tokens of one block no expert is named more than 48 times, and in some block some expert is named exactly 48 times.
All inputs are finite; a program needn't handle non-finite values.
Results may differ from a plain program's by a relative error of at most 0.02.
Values may be sent and summed in bfloat16 or wider, within the bound.
A program may use at most 128 MiB of HBM per device.

v0:
```python
import jax
import jax.numpy as jnp
from jax import lax
from jax.sharding import PartitionSpec as P


def slot_table(assignment, groups, capacity):
    flat = assignment.reshape(-1)
    onehot = (flat[:, None] == jnp.arange(groups, dtype=jnp.int32)[None, :]).astype(jnp.int32)
    before = jnp.cumsum(onehot, axis=0) - onehot
    position = jnp.sum(before * onehot, axis=1)
    return (flat * capacity + position).reshape(assignment.shape)


def front_half(gathered, gate_local, up_local):
    pre_gate = jnp.dot(gathered, gate_local, preferred_element_type=jnp.float32)
    pre_up = jnp.dot(gathered, up_local, preferred_element_type=jnp.float32)
    sigma = jax.nn.sigmoid(pre_gate)
    silu_gate = pre_gate * sigma
    hidden = (silu_gate * pre_up).astype(jnp.bfloat16)
    return (pre_gate, pre_up, sigma, silu_gate, hidden)


def spread(buffer, groups, capacity):
    width = buffer.shape[-1]
    blocks = buffer.reshape(groups, capacity, width)
    arrived = lax.all_to_all(blocks, "expert", split_axis=0, concat_axis=0, tiled=True)
    return arrived.reshape(-1, width)


def return_rows(term_fn, rows, groups, capacity, width):
    shares = lax.psum_scatter(
        term_fn(jnp.int32(0), rows * lax.axis_size("fsdp")).astype(jnp.bfloat16),
        "fsdp",
        scatter_dimension=0,
        tiled=True,
    )
    summed = lax.all_gather(shares, "fsdp", axis=0, tiled=True)
    back = lax.all_to_all(
        summed.reshape(groups, capacity, width), "expert", split_axis=0, concat_axis=0, tiled=True
    )
    return back.reshape(-1, width)


def per_device(tokens, assignment, route_weight, cotangent, w_gate, w_up, w_down):
    tok_dev = tokens.shape[0]
    width = tokens.shape[1]
    groups = lax.axis_size("expert")
    capacity = max(2, 3 * tok_dev // groups)
    slot_count = groups * capacity
    share_rows = slot_count // lax.axis_size("fsdp")
    table = slot_table(assignment, groups, capacity)
    slot_ids = jnp.arange(slot_count, dtype=jnp.int32)
    pick_first = slot_ids[:, None] == table[:, 0][None, :]
    pick_second = slot_ids[:, None] == table[:, 1][None, :]
    pick_both = jnp.logical_or(pick_first, pick_second).astype(jnp.bfloat16)
    sent_tokens = jnp.dot(pick_both, tokens, preferred_element_type=jnp.float32).astype(
        jnp.bfloat16
    )
    weighted = (route_weight[:, :, None] * cotangent[:, None, :].astype(jnp.float32)).astype(
        jnp.bfloat16
    )
    sent_cot = (
        jnp.dot(pick_first.astype(jnp.bfloat16), weighted[:, 0], preferred_element_type=jnp.float32)
        + jnp.dot(
            pick_second.astype(jnp.bfloat16), weighted[:, 1], preferred_element_type=jnp.float32
        )
    ).astype(jnp.bfloat16)
    gate_local = w_gate[0]
    up_local = w_up[0]
    down_local = w_down[0]
    gathered = spread(sent_tokens, groups, capacity)
    pre_gate, pre_up, sigma, silu_gate, hidden = front_half(gathered, gate_local, up_local)

    def out_term(start, count):
        return jnp.dot(hidden, down_local, preferred_element_type=jnp.float32)

    out_back = return_rows(out_term, share_rows, groups, capacity, width).astype(jnp.float32)
    select_first = pick_first.astype(jnp.float32)
    select_second = pick_second.astype(jnp.float32)
    first_out = jnp.dot(select_first.T, out_back, precision=lax.Precision.HIGHEST)
    second_out = jnp.dot(select_second.T, out_back, precision=lax.Precision.HIGHEST)
    moe_out = (route_weight[:, 0:1] * first_out + route_weight[:, 1:2] * second_out).astype(
        jnp.bfloat16
    )
    cot_float = cotangent.astype(jnp.float32)
    grad_prob = jnp.stack(
        [jnp.sum(cot_float * first_out, axis=1), jnp.sum(cot_float * second_out, axis=1)], axis=1
    )
    grad_gathered = spread(sent_cot, groups, capacity)
    grad_hidden = jnp.dot(grad_gathered, down_local.T, preferred_element_type=jnp.float32)
    grad_down = jnp.dot(hidden.T, grad_gathered, preferred_element_type=jnp.float32).astype(
        jnp.bfloat16
    )
    grad_pre_gate = (grad_hidden * pre_up * sigma * (1.0 + pre_gate * (1.0 - sigma))).astype(
        jnp.bfloat16
    )
    grad_pre_up = (grad_hidden * silu_gate).astype(jnp.bfloat16)
    grad_gate = jnp.dot(gathered.T, grad_pre_gate, preferred_element_type=jnp.float32).astype(
        jnp.bfloat16
    )
    grad_up = jnp.dot(gathered.T, grad_pre_up, preferred_element_type=jnp.float32).astype(
        jnp.bfloat16
    )

    def back_term(start, count):
        return jnp.dot(grad_pre_gate, gate_local.T, preferred_element_type=jnp.float32) + jnp.dot(
            grad_pre_up, up_local.T, preferred_element_type=jnp.float32
        )

    grad_back = return_rows(back_term, share_rows, groups, capacity, width).astype(jnp.float32)
    grad_tokens = (
        jnp.dot(select_first.T, grad_back, precision=lax.Precision.HIGHEST)
        + jnp.dot(select_second.T, grad_back, precision=lax.Precision.HIGHEST)
    ).astype(jnp.bfloat16)
    return (moe_out, grad_tokens, grad_prob, grad_gate[None], grad_up[None], grad_down[None])


def solution(mesh):
    return jax.shard_map(
        per_device,
        mesh=mesh,
        in_specs=(
            P("expert", None),
            P("expert", None),
            P("expert", None),
            P("expert", None),
            P("expert", None, "fsdp"),
            P("expert", None, "fsdp"),
            P("expert", "fsdp", None),
        ),
        out_specs=(
            P("expert", None),
            P("expert", None),
            P("expert", None),
            P("expert", None, "fsdp"),
            P("expert", None, "fsdp"),
            P("expert", "fsdp", None),
        ),
        check_vma=False,
    )
```

profile of v0, /device:TPU:6, one launch (start us, length us, event | category | flops | bytes accessed | tf_op | source)
XLA Modules:
  0.0 465.9 jit_solution(11138213794973551333)
XLA Ops:
  13.6 6.6 %all-to-all-start = ((bf16[8,48,3072]{2,1,0:T(8,128)(2,1)}), bf16[8,48,3072]{2,1,0:T(8,128)(2,1)}, u32[]{:S(2)}, u32[]{:S(2)}) async-start(bf16[8,48,3072]{2,1,0:T(8,128)(2,1)} %bitcast.80), calls=%async_computation | async-start | bytes 4718592 | tf_op jit(solution)/shard_map/all_to_all | solution.py:27
  23.6 25.5 %all-to-all-done = bf16[8,48,3072]{2,1,0:T(8,128)(2,1)} async-done(((bf16[8,48,3072]{2,1,0:T(8,128)(2,1)}), bf16[8,48,3072]{2,1,0:T(8,128)(2,1)}, u32[]{:S(2)}, u32[]{:S(2)}) %all-to-all-start) | async-done | bytes 2359328 | tf_op jit(solution)/shard_map/all_to_all | solution.py:27
  49.1 5.4 %all-to-all-start.2 = ((bf16[8,48,3072]{2,1,0:T(8,128)(2,1)}), bf16[8,48,3072]{2,1,0:T(8,128)(2,1)}, u32[]{:S(2)}, u32[]{:S(2)}) async-start(bf16[8,48,3072]{2,1,0:T(8,128)(2,1)} %bitcast.81), calls=%async_computation.2 | async-start | bytes 4718592 | tf_op jit(solution)/shard_map/all_to_all | solution.py:27
  61.5 21.2 %all-to-all-done.2 = bf16[8,48,3072]{2,1,0:T(8,128)(2,1)} async-done(((bf16[8,48,3072]{2,1,0:T(8,128)(2,1)}), bf16[8,48,3072]{2,1,0:T(8,128)(2,1)}, u32[]{:S(2)}, u32[]{:S(2)}) %all-to-all-start.2) | async-done | bytes 2359328 | tf_op jit(solution)/shard_map/all_to_all | solution.py:27
  90.8 86.6 %fusion.34 = (bf16[16,3072]{1,0:T(8,128)(2,1)S(1)}, bf16[16,3072]{1,0:T(8,128)(2,1)S(1)}) fusion(bf16[384,3072]{1,0:T(8,128)(2,1)} %convolution_convert_fusion.1, bf16[384,3072]{1,0:T(8,128)(2,1)} %add_convert_fusion), kind=kCustom, calls=%all-reduce-scatter.2 | all-reduce-scatter fusion | flops 3145729 | bytes 4916224
  182.7 10.9 %collective-permute-start.3 = (bf16[16,3072]{1,0:T(8,128)(2,1)S(1)}, bf16[16,3072]{1,0:T(8,128)(2,1)S(1)}, u32[]{:S(2)}, u32[]{:S(2)}) collective-permute-start(bf16[16,3072]{1,0:T(8,128)(2,1)S(1)} %get-tuple-element.10), channel_id=1, source_target_pairs={{0,4},{1,5},{2,6},{3,7},{4,8},{5,9},{6,10},{7,11},{8,12},{9,13},{1... | collective-permute-start | bytes 294920
  198.1 5.3 %collective-permute-start.6 = (bf16[16,3072]{1,0:T(8,128)(2,1)S(1)}, bf16[16,3072]{1,0:T(8,128)(2,1)}, u32[]{:S(2)}, u32[]{:S(2)}) collective-permute-start(bf16[16,3072]{1,0:T(8,128)(2,1)S(1)} %get-tuple-element.10), channel_id=1, source_target_pairs={{0,7},{1,8},{2,9},{3,10},{4,11},{5,12},{6,13},{7,14},{8,15},{9,16}... | collective-permute-start | bytes 294920
  204.7 4.6 collective-permute-done.5
  209.9 4.3 collective-permute-done.6
  214.2 6.5 %concatenate = bf16[140,3072]{1,0:T(8,128)(2,1)S(1)} concatenate(bf16[12,3072]{1,0:T(8,128)(2,1)S(1)} %collective-permute-done.7, bf16[16,3072]{1,0:T(8,128)(2,1)} %collective-permute-done.6, bf16[16,3072]{1,0:T(8,128)(2,1)} %copy-done.8, bf16[16,3072]{1,0:T(8,128)(2,1)} %copy-done.7, bf16[16,3072]{1,0:T(8,128)(2,1)S(1)} %collective-permute-done.3, ...), dimensions={0} | concatenate | bytes 1720320
  222.8 6.9 %collective-permute-start.11 = (bf16[16,3072]{1,0:T(8,128)(2,1)S(1)}, bf16[16,3072]{1,0:T(8,128)(2,1)S(1)}, u32[]{:S(2)}, u32[]{:S(2)}) collective-permute-start(bf16[16,3072]{1,0:T(8,128)(2,1)S(1)} %get-tuple-element.11), channel_id=1, source_target_pairs={{0,4},{1,5},{2,6},{3,7},{4,8},{5,9},{6,10},{7,11},{8,12},{9,13},{1... | collective-permute-start | bytes 294920
  229.7 4.3 collective-permute-start.15
  234.0 7.4 %collective-permute-start.12 = (bf16[16,3072]{1,0:T(8,128)(2,1)S(1)}, bf16[16,3072]{1,0:T(8,128)(2,1)S(1)}, u32[]{:S(2)}, u32[]{:S(2)}) collective-permute-start(bf16[16,3072]{1,0:T(8,128)(2,1)S(1)} %get-tuple-element.11), channel_id=1, source_target_pairs={{0,5},{1,6},{2,7},{3,8},{4,9},{5,10},{6,11},{7,12},{8,13},{9,14},{... | collective-permute-start | bytes 294920
  247.6 6.7 %collective-permute-start.9 = (bf16[16,3072]{1,0:T(8,128)(2,1)S(1)}, bf16[16,3072]{1,0:T(8,128)(2,1)}, u32[]{:S(2)}, u32[]{:S(2)}) collective-permute-start(bf16[16,3072]{1,0:T(8,128)(2,1)S(1)} %get-tuple-element.11), channel_id=1, source_target_pairs={{0,2},{1,3},{2,4},{3,5},{4,6},{5,7},{6,8},{7,9},{8,10},{9,11},{10,... | collective-permute-start | bytes 294920
  264.3 5.1 %concatenate.1 = bf16[140,3072]{1,0:T(8,128)(2,1)S(1)} concatenate(bf16[12,3072]{1,0:T(8,128)(2,1)S(1)} %collective-permute-done.15, bf16[16,3072]{1,0:T(8,128)(2,1)S(1)} %collective-permute-done.14, bf16[16,3072]{1,0:T(8,128)(2,1)S(1)} %collective-permute-done.13, bf16[16,3072]{1,0:T(8,128)(2,1)S(1)} %collective-permute-done.12, bf16[16,3072]{1,0:T(8,128)(2,1)S(1)} %collective-permute-done.11, ...), dimensions={0} | concatenate | bytes 1720320
  270.1 39.0 %all-gather.5.cloned.1.call-done = bf16[32,12,3072]{2,1,0:T(8,128)(2,1)} async-done(((bf16[1,12,3072]{2,1,0:T(8,128)(2,1)}), bf16[32,12,3072]{2,1,0:T(8,128)(2,1)}) %all-gather.5.cloned.1.call-update) | async-done | bytes 2359312 | tf_op jit(solution)/shard_map/all_gather | solution.py:38
  309.0 4.3 reshape.64
  313.3 4.8 %all-to-all-start.1 = ((bf16[8,48,3072]{2,1,0:T(8,128)(2,1)}), bf16[8,48,3072]{2,1,0:T(8,128)(2,1)}, u32[]{:S(2)}, u32[]{:S(2)}) async-start(bf16[8,48,3072]{2,1,0:T(8,128)(2,1)} %reshape.64), calls=%async_computation.1 | async-start | bytes 4718592 | tf_op jit(solution)/shard_map/all_to_all | solution.py:39
  318.1 87.1 %all-gather.7.cloned.1.call-done = bf16[32,12,3072]{2,1,0:T(8,128)(2,1)} async-done(((bf16[1,12,3072]{2,1,0:T(8,128)(2,1)}), bf16[32,12,3072]{2,1,0:T(8,128)(2,1)}) %all-gather.7.cloned.1.call-update) | async-done | bytes 2359312 | tf_op jit(solution)/shard_map/all_gather | solution.py:38
  405.3 4.2 reshape.68
  409.5 4.8 %all-to-all-start.3 = ((bf16[8,48,3072]{2,1,0:T(8,128)(2,1)}), bf16[8,48,3072]{2,1,0:T(8,128)(2,1)}, u32[]{:S(2)}, u32[]{:S(2)}) async-start(bf16[8,48,3072]{2,1,0:T(8,128)(2,1)} %reshape.68), calls=%async_computation.3 | async-start | bytes 4718592 | tf_op jit(solution)/shard_map/all_to_all | solution.py:39
  418.7 3.9 fusion.2
  422.5 3.8 fusion.3
  428.7 20.8 %all-to-all-done.3 = bf16[8,48,3072]{2,1,0:T(8,128)(2,1)} async-done(((bf16[8,48,3072]{2,1,0:T(8,128)(2,1)}), bf16[8,48,3072]{2,1,0:T(8,128)(2,1)}, u32[]{:S(2)}, u32[]{:S(2)}) %all-to-all-start.3) | async-done | bytes 2359328 | tf_op jit(solution)/shard_map/all_to_all | solution.py:39
  (91 shorter events, 70.9 us)
Async XLA Ops:
  7.2 75.6 %copy-start = (bf16[1,256,3072]{2,1,0:T(8,128)(2,1)S(1)}, bf16[1,256,3072]{2,1,0:T(8,128)(2,1)}, u32[]{:S(2)}) copy-start(bf16[1,256,3072]{2,1,0:T(8,128)(2,1)} %param.13) | copy-start | bytes 4718596
  13.6 35.6 %all-to-all-start = ((bf16[8,48,3072]{2,1,0:T(8,128)(2,1)}), bf16[8,48,3072]{2,1,0:T(8,128)(2,1)}, u32[]{:S(2)}, u32[]{:S(2)}) async-start(bf16[8,48,3072]{2,1,0:T(8,128)(2,1)} %bitcast.80), calls=%async_computation | async-start | bytes 4718592 | tf_op jit(solution)/shard_map/all_to_all | solution.py:27
  49.1 33.6 %all-to-all-start.2 = ((bf16[8,48,3072]{2,1,0:T(8,128)(2,1)}), bf16[8,48,3072]{2,1,0:T(8,128)(2,1)}, u32[]{:S(2)}, u32[]{:S(2)}) async-start(bf16[8,48,3072]{2,1,0:T(8,128)(2,1)} %bitcast.81), calls=%async_computation.2 | async-start | bytes 4718592 | tf_op jit(solution)/shard_map/all_to_all | solution.py:27
  54.6 254.5 %all-gather.5.cloned.1.call-start = ((), (), s32[]{:S(2)}) async-start(), calls=%async_computation.4 | async-start | bytes 3244032 | tf_op jit(solution)/shard_map/all_gather | solution.py:38
  90.8 112.6 %copy-start.12 = (u32[256]{0:T(256)S(1)}, u32[256]{0:T(256)}, u32[]{:S(2)}) copy-start(u32[256]{0:T(256)} %constant.17) | copy-start | bytes 3076
  177.4 17.9 %collective-permute-start = (bf16[16,3072]{1,0:T(8,128)(2,1)S(1)}, bf16[16,3072]{1,0:T(8,128)(2,1)S(1)}, u32[]{:S(2)}, u32[]{:S(2)}) collective-permute-start(bf16[16,3072]{1,0:T(8,128)(2,1)S(1)} %get-tuple-element.10), channel_id=1, source_target_pairs={{0,1},{1,2},{2,3},{3,4},{4,5},{5,6},{6,7},{7,8},{8,9},{9,10},{10,1... | collective-permute-start | bytes 294920
  178.7 19.3 %collective-permute-start.1 = (bf16[16,3072]{1,0:T(8,128)(2,1)S(1)}, bf16[16,3072]{1,0:T(8,128)(2,1)S(1)}, u32[]{:S(2)}, u32[]{:S(2)}) collective-permute-start(bf16[16,3072]{1,0:T(8,128)(2,1)S(1)} %get-tuple-element.10), channel_id=1, source_target_pairs={{0,2},{1,3},{2,4},{3,5},{4,6},{5,7},{6,8},{7,9},{8,10},{9,11},{10,... | collective-permute-start | bytes 294920
  180.1 13.6 %collective-permute-start.7 = (bf16[12,3072]{1,0:T(8,128)(2,1)S(1)}, bf16[12,3072]{1,0:T(8,128)(2,1)S(1)}, u32[]{:S(2)}, u32[]{:S(2)}) collective-permute-start(bf16[12,3072]{1,0:T(8,128)(2,1)S(1)} %slice.35), channel_id=1, source_target_pairs={{0,8},{1,9},{2,10},{3,11},{4,12},{5,13},{6,14},{7,15},{8,16},{9,17... | collective-permute-start | bytes 221192
  181.4 23.3 %collective-permute-start.2 = (bf16[16,3072]{1,0:T(8,128)(2,1)S(1)}, bf16[16,3072]{1,0:T(8,128)(2,1)S(1)}, u32[]{:S(2)}, u32[]{:S(2)}) collective-permute-start(bf16[16,3072]{1,0:T(8,128)(2,1)S(1)} %get-tuple-element.10), channel_id=1, source_target_pairs={{0,3},{1,4},{2,5},{3,6},{4,7},{5,8},{6,9},{7,10},{8,11},{9,12},{10... | collective-permute-start | bytes 294920
  182.7 22.0 %collective-permute-start.3 = (bf16[16,3072]{1,0:T(8,128)(2,1)S(1)}, bf16[16,3072]{1,0:T(8,128)(2,1)S(1)}, u32[]{:S(2)}, u32[]{:S(2)}) collective-permute-start(bf16[16,3072]{1,0:T(8,128)(2,1)S(1)} %get-tuple-element.10), channel_id=1, source_target_pairs={{0,4},{1,5},{2,6},{3,7},{4,8},{5,9},{6,10},{7,11},{8,12},{9,13},{1... | collective-permute-start | bytes 294920
  193.6 11.0 %collective-permute-start.4 = (bf16[16,3072]{1,0:T(8,128)(2,1)S(1)}, bf16[16,3072]{1,0:T(8,128)(2,1)S(1)}, u32[]{:S(2)}, u32[]{:S(2)}) collective-permute-start(bf16[16,3072]{1,0:T(8,128)(2,1)S(1)} %get-tuple-element.10), channel_id=1, source_target_pairs={{0,5},{1,6},{2,7},{3,8},{4,9},{5,10},{6,11},{7,12},{8,13},{9,14},{... | collective-permute-start | bytes 294920
  195.3 13.9 %collective-permute-start.5 = (bf16[16,3072]{1,0:T(8,128)(2,1)S(1)}, bf16[16,3072]{1,0:T(8,128)(2,1)S(1)}, u32[]{:S(2)}, u32[]{:S(2)}) collective-permute-start(bf16[16,3072]{1,0:T(8,128)(2,1)S(1)} %get-tuple-element.10), channel_id=1, source_target_pairs={{0,6},{1,7},{2,8},{3,9},{4,10},{5,11},{6,12},{7,13},{8,14},{9,15},... | collective-permute-start | bytes 294920
  198.1 16.1 %collective-permute-start.6 = (bf16[16,3072]{1,0:T(8,128)(2,1)S(1)}, bf16[16,3072]{1,0:T(8,128)(2,1)}, u32[]{:S(2)}, u32[]{:S(2)}) collective-permute-start(bf16[16,3072]{1,0:T(8,128)(2,1)S(1)} %get-tuple-element.10), channel_id=1, source_target_pairs={{0,7},{1,8},{2,9},{3,10},{4,11},{5,12},{6,13},{7,14},{8,15},{9,16}... | collective-permute-start | bytes 294920
  221.4 183.9 %all-gather.7.cloned.1.call-start = ((), (), s32[]{:S(2)}) async-start(), calls=%async_computation.5 | async-start | bytes 3244032 | tf_op jit(solution)/shard_map/all_gather | solution.py:38
  221.5 24.1 %collective-permute-start.10 = (bf16[16,3072]{1,0:T(8,128)(2,1)S(1)}, bf16[16,3072]{1,0:T(8,128)(2,1)S(1)}, u32[]{:S(2)}, u32[]{:S(2)}) collective-permute-start(bf16[16,3072]{1,0:T(8,128)(2,1)S(1)} %get-tuple-element.11), channel_id=1, source_target_pairs={{0,3},{1,4},{2,5},{3,6},{4,7},{5,8},{6,9},{7,10},{8,11},{9,12},{10... | collective-permute-start | bytes 294920
  222.8 24.8 %collective-permute-start.11 = (bf16[16,3072]{1,0:T(8,128)(2,1)S(1)}, bf16[16,3072]{1,0:T(8,128)(2,1)S(1)}, u32[]{:S(2)}, u32[]{:S(2)}) collective-permute-start(bf16[16,3072]{1,0:T(8,128)(2,1)S(1)} %get-tuple-element.11), channel_id=1, source_target_pairs={{0,4},{1,5},{2,6},{3,7},{4,8},{5,9},{6,10},{7,11},{8,12},{9,13},{1... | collective-permute-start | bytes 294920
  229.7 13.0 %collective-permute-start.15 = (bf16[12,3072]{1,0:T(8,128)(2,1)S(1)}, bf16[12,3072]{1,0:T(8,128)(2,1)S(1)}, u32[]{:S(2)}, u32[]{:S(2)}) collective-permute-start(bf16[12,3072]{1,0:T(8,128)(2,1)S(1)} %slice.36), channel_id=1, source_target_pairs={{0,8},{1,9},{2,10},{3,11},{4,12},{5,13},{6,14},{7,15},{8,16},{9,17... | collective-permute-start | bytes 221192
  234.0 20.3 %collective-permute-start.12 = (bf16[16,3072]{1,0:T(8,128)(2,1)S(1)}, bf16[16,3072]{1,0:T(8,128)(2,1)S(1)}, u32[]{:S(2)}, u32[]{:S(2)}) collective-permute-start(bf16[16,3072]{1,0:T(8,128)(2,1)S(1)} %get-tuple-element.11), channel_id=1, source_target_pairs={{0,5},{1,6},{2,7},{3,8},{4,9},{5,10},{6,11},{7,12},{8,13},{9,14},{... | collective-permute-start | bytes 294920
  241.4 16.4 %collective-permute-start.13 = (bf16[16,3072]{1,0:T(8,128)(2,1)S(1)}, bf16[16,3072]{1,0:T(8,128)(2,1)S(1)}, u32[]{:S(2)}, u32[]{:S(2)}) collective-permute-start(bf16[16,3072]{1,0:T(8,128)(2,1)S(1)} %get-tuple-element.11), channel_id=1, source_target_pairs={{0,6},{1,7},{2,8},{3,9},{4,10},{5,11},{6,12},{7,13},{8,14},{9,15},... | collective-permute-start | bytes 294920
  242.7 18.3 %collective-permute-start.14 = (bf16[16,3072]{1,0:T(8,128)(2,1)S(1)}, bf16[16,3072]{1,0:T(8,128)(2,1)S(1)}, u32[]{:S(2)}, u32[]{:S(2)}) collective-permute-start(bf16[16,3072]{1,0:T(8,128)(2,1)S(1)} %get-tuple-element.11), channel_id=1, source_target_pairs={{0,7},{1,8},{2,9},{3,10},{4,11},{5,12},{6,13},{7,14},{8,15},{9,16}... | collective-permute-start | bytes 294920
  245.5 15.5 %collective-permute-start.8 = (bf16[16,3072]{1,0:T(8,128)(2,1)S(1)}, bf16[16,3072]{1,0:T(8,128)(2,1)S(1)}, u32[]{:S(2)}, u32[]{:S(2)}) collective-permute-start(bf16[16,3072]{1,0:T(8,128)(2,1)S(1)} %get-tuple-element.11), channel_id=1, source_target_pairs={{0,1},{1,2},{2,3},{3,4},{4,5},{5,6},{6,7},{7,8},{8,9},{9,10},{10,1... | collective-permute-start | bytes 294920
  247.6 16.7 %collective-permute-start.9 = (bf16[16,3072]{1,0:T(8,128)(2,1)S(1)}, bf16[16,3072]{1,0:T(8,128)(2,1)}, u32[]{:S(2)}, u32[]{:S(2)}) collective-permute-start(bf16[16,3072]{1,0:T(8,128)(2,1)S(1)} %get-tuple-element.11), channel_id=1, source_target_pairs={{0,2},{1,3},{2,4},{3,5},{4,6},{5,7},{6,8},{7,9},{8,10},{9,11},{10,... | collective-permute-start | bytes 294920
  313.3 96.2 %all-to-all-start.1 = ((bf16[8,48,3072]{2,1,0:T(8,128)(2,1)}), bf16[8,48,3072]{2,1,0:T(8,128)(2,1)}, u32[]{:S(2)}, u32[]{:S(2)}) async-start(bf16[8,48,3072]{2,1,0:T(8,128)(2,1)} %reshape.64), calls=%async_computation.1 | async-start | bytes 4718592 | tf_op jit(solution)/shard_map/all_to_all | solution.py:39
  409.5 39.9 %all-to-all-start.3 = ((bf16[8,48,3072]{2,1,0:T(8,128)(2,1)}), bf16[8,48,3072]{2,1,0:T(8,128)(2,1)}, u32[]{:S(2)}, u32[]{:S(2)}) async-start(bf16[8,48,3072]{2,1,0:T(8,128)(2,1)} %reshape.68), calls=%async_computation.3 | async-start | bytes 4718592 | tf_op jit(solution)/shard_map/all_to_all | solution.py:39
  (11 other events, 38.7 us)
Sparse Core Ops, SparseCore 0:
  221.5 87.4 all-gather.4
  312.4 92.8 all-gather.6
where the time goes:
time: 468 us; the launch traced here: 466 us
  waiting for transfers between devices  212 us (45%)
  blocking collectives  86.6 us (19%)
  starting transfers between devices  80.2 us (17%)
  matrix products  44.2 us (9%)
  local copies, waits for them, and re-layouts  25.5 us (5%)
  between operations  15.1 us (3%)
    all_gather x2, waiting for transfers between devices, return_rows(): summed = lax.all_gather(shares, 'fsdp', axis=0, tiled=True)  126 us
    unnamed x1, blocking collectives  86.6 us
    unnamed x16, starting transfers between devices  58.5 us
    all_to_all x2, waiting for transfers between devices, spread(): lax.all_to_all(blocks, 'expert', split_axis=0, concat_axis=0, tiled=True)  46.7 us
    all_to_all x2, waiting for transfers between devices, return_rows(): lax.all_to_all(summed.reshape(groups, capacity, width), 'expert', split_a...  20.8 us
    unnamed x18, waiting for transfers between devices  18.3 us
    unnamed x34, local copies, waits for them, and re-layouts  15.8 us
    all_to_all x2, starting transfers between devices, spread(): lax.all_to_all(blocks, 'expert', split_axis=0, concat_axis=0, tiled=True)  12 us
  transfers between devices with their start and end apart: 22, of which 10 were waited for; matrix products, arithmetic and copies ran while one was open for 8% of the time, Pallas kernels for 0%

commit v1 on v0

--- a/solution.py
+++ b/solution.py
@@ -2,6 +2,15 @@
 import jax.numpy as jnp
 from jax import lax
 from jax.sharding import PartitionSpec as P
+
+
+def save_shapes(x_in):
+    return jnp.concatenate(
+        lax.all_to_all(
+            jnp.stack([x_in for _ in range(lax.axis_size("fsdp"))], axis=0), "fsdp", 0, 0
+        ),
+        axis=0,
+    )
 
 
 def slot_table(assignment, groups, capacity):
@@ -35,7 +44,7 @@
         scatter_dimension=0,
         tiled=True,
     )
-    summed = lax.all_gather(shares, "fsdp", axis=0, tiled=True)
+    summed = save_shapes(shares)
     back = lax.all_to_all(
         summed.reshape(groups, capacity, width), "expert", split_axis=0, concat_axis=0, tiled=True
     )

time: 468 us -> 515 us (1.10)
  starting transfers between devices: 80.2 us -> 111 us
  waiting for transfers between devices: 212 us -> 230 us
  between operations: 15.1 us -> 1.74 us
  local copies, waits for them, and re-layouts: 25.5 us -> 37.8 us
    all_gather x2 -> x0, waiting for transfers between devices: 126 us -> none  [return_rows(): summed = lax.all_gather(shares, 'fsdp', axis=0, tiled=True)]
    all_to_all x0 -> x2, waiting for transfers between devices: none -> 72.1 us  [save_shapes(): lax.all_to_all(jnp.stack([x_in for _ in range(lax.axis_size('fsdp'))], ax...]
    unnamed x18 -> x16, waiting for transfers between devices: 18.3 us -> 68.6 us
    all_to_all x0 -> x2, starting transfers between devices: none -> 24.8 us  [save_shapes(): lax.all_to_all(jnp.stack([x_in for _ in range(lax.axis_size('fsdp'))], ax...]
    all_to_all x2, waiting for transfers between devices: 20.8 us -> 41.7 us  [return_rows(): lax.all_to_all(summed.reshape(groups, capacity, width), 'expert', split_a...]
    unnamed x34 -> x52, local copies, waits for them, and re-layouts: 15.8 us -> 26.6 us
    another operation x1 -> x5, local copies, waits for them, and re-layouts: 0.01 us -> 10.5 us  [the longest x2 6.41 us: return_rows(): summed.reshape(groups, capacity, width)]
    reshape x2 -> x0, local copies, waits for them, and re-layouts: 8.5 us -> none  [return_rows(): summed.reshape(groups, capacity, width)]
  transfers between devices with their start and end apart: 22 -> 22, of which waited for: 10 -> 10; matrix products, arithmetic and copies ran while one was open for 8% -> 10% of each run, Pallas kernels for 0% -> 0%
where the time goes in v1:
time: 515 us; the launch traced here: 511 us
  waiting for transfers between devices  230 us (45%)
  starting transfers between devices  111 us (22%)
  blocking collectives  86 us (17%)
  matrix products  42.1 us (8%)
  local copies, waits for them, and re-layouts  37.8 us (7%)
    unnamed x1, blocking collectives  86 us
    all_to_all x2, waiting for transfers between devices, save_shapes(): lax.all_to_all(jnp.stack([x_in for _ in range(lax.axis_size('fsdp'))], ax...  72.1 us
    unnamed x16, waiting for transfers between devices  68.6 us
    unnamed x16, starting transfers between devices  62.7 us
    all_to_all x2, waiting for transfers between devices, spread(): lax.all_to_all(blocks, 'expert', split_axis=0, concat_axis=0, tiled=True)  47.4 us
    all_to_all x2, waiting for transfers between devices, return_rows(): lax.all_to_all(summed.reshape(groups, capacity, width), 'expert', split_a...  41.7 us
    unnamed x52, local copies, waits for them, and re-layouts  26.6 us
    all_to_all x2, starting transfers between devices, save_shapes(): lax.all_to_all(jnp.stack([x_in for _ in range(lax.axis_size('fsdp'))], ax...  24.8 us
  transfers between devices with their start and end apart: 22, of which 10 were waited for; matrix products, arithmetic and copies ran while one was open for 10% of the time, Pallas kernels for 0%

profile of v1, /device:TPU:6, one launch (start us, length us, event | category | flops | bytes accessed | tf_op | source)
XLA Modules:
  0.0 510.7 jit_solution(2699267608159276541)
XLA Ops:
  7.0 6.6 %all-to-all-start = ((bf16[8,48,3072]{2,1,0:T(8,128)(2,1)}), bf16[8,48,3072]{2,1,0:T(8,128)(2,1)}, u32[]{:S(2)}, u32[]{:S(2)}) async-start(bf16[8,48,3072]{2,1,0:T(8,128)(2,1)} %bitcast.78), calls=%async_computation | async-start | bytes 4718592 | tf_op jit(solution)/shard_map/all_to_all | solution.py:36
  17.1 25.5 %all-to-all-done = bf16[8,48,3072]{2,1,0:T(8,128)(2,1)} async-done(((bf16[8,48,3072]{2,1,0:T(8,128)(2,1)}), bf16[8,48,3072]{2,1,0:T(8,128)(2,1)}, u32[]{:S(2)}, u32[]{:S(2)}) %all-to-all-start) | async-done | bytes 2359328 | tf_op jit(solution)/shard_map/all_to_all | solution.py:36
  42.6 5.4 %all-to-all-start.3 = ((bf16[8,48,3072]{2,1,0:T(8,128)(2,1)}), bf16[8,48,3072]{2,1,0:T(8,128)(2,1)}, u32[]{:S(2)}, u32[]{:S(2)}) async-start(bf16[8,48,3072]{2,1,0:T(8,128)(2,1)} %bitcast.79), calls=%async_computation.3 | async-start | bytes 4718592 | tf_op jit(solution)/shard_map/all_to_all | solution.py:36
  54.9 21.9 %all-to-all-done.3 = bf16[8,48,3072]{2,1,0:T(8,128)(2,1)} async-done(((bf16[8,48,3072]{2,1,0:T(8,128)(2,1)}), bf16[8,48,3072]{2,1,0:T(8,128)(2,1)}, u32[]{:S(2)}, u32[]{:S(2)}) %all-to-all-start.3) | async-done | bytes 2359328 | tf_op jit(solution)/shard_map/all_to_all | solution.py:36
  84.8 86.0 %fusion.34 = (bf16[16,3072]{1,0:T(8,128)(2,1)S(1)}, bf16[16,3072]{1,0:T(8,128)(2,1)S(1)}) fusion(bf16[384,3072]{1,0:T(8,128)(2,1)S(1)} %copy-done.4, bf16[384,3072]{1,0:T(8,128)(2,1)} %add_convert_fusion), kind=kCustom, calls=%all-reduce-scatter.2 | all-reduce-scatter fusion | flops 3145729 | bytes 4916224
  176.1 10.9 %collective-permute-start.3 = (bf16[16,3072]{1,0:T(8,128)(2,1)S(1)}, bf16[16,3072]{1,0:T(8,128)(2,1)S(1)}, u32[]{:S(2)}, u32[]{:S(2)}) collective-permute-start(bf16[16,3072]{1,0:T(8,128)(2,1)S(1)} %get-tuple-element.10), channel_id=1, source_target_pairs={{0,4},{1,5},{2,6},{3,7},{4,8},{5,9},{6,10},{7,11},{8,12},{9,13},{1... | collective-permute-start | bytes 294920
  191.5 4.7 collective-permute-start.6
  197.5 5.2 %collective-permute-done.5 = bf16[16,3072]{1,0:T(8,128)(2,1)S(1)} collective-permute-done((bf16[16,3072]{1,0:T(8,128)(2,1)S(1)}, bf16[16,3072]{1,0:T(8,128)(2,1)S(1)}, u32[]{:S(2)}, u32[]{:S(2)}) %collective-permute-start.5) | collective-permute-done | bytes 98336
  202.6 4.9 collective-permute-done.6
  211.7 8.4 %all-to-all-start.1 = ((bf16[32,12,3072]{2,1,0:T(8,128)(2,1)}), bf16[32,12,3072]{2,1,0:T(8,128)(2,1)S(1)}, u32[]{:S(2)}, u32[]{:S(2)}) async-start(bf16[32,12,3072]{2,1,0:T(8,128)(2,1)} %stack.10), calls=%async_computation.1 | async-start | bytes 6291456 | tf_op jit(solution)/shard_map/all_to_all | solution.py:9
  223.6 4.3 collective-permute-start.11
  227.9 4.6 collective-permute-start.15
  232.5 6.1 %collective-permute-start.12 = (bf16[16,3072]{1,0:T(8,128)(2,1)S(1)}, bf16[16,3072]{1,0:T(8,128)(2,1)S(1)}, u32[]{:S(2)}, u32[]{:S(2)}) collective-permute-start(bf16[16,3072]{1,0:T(8,128)(2,1)S(1)} %get-tuple-element.11), channel_id=1, source_target_pairs={{0,5},{1,6},{2,7},{3,8},{4,9},{5,10},{6,11},{7,12},{8,13},{9,14},{... | collective-permute-start | bytes 294920
  238.6 5.5 %collective-permute-start.13 = (bf16[16,3072]{1,0:T(8,128)(2,1)S(1)}, bf16[16,3072]{1,0:T(8,128)(2,1)S(1)}, u32[]{:S(2)}, u32[]{:S(2)}) collective-permute-start(bf16[16,3072]{1,0:T(8,128)(2,1)S(1)} %get-tuple-element.11), channel_id=1, source_target_pairs={{0,6},{1,7},{2,8},{3,9},{4,10},{5,11},{6,12},{7,13},{8,14},{9,15},... | collective-permute-start | bytes 294920
  244.2 57.2 %collective-permute-done.15 = bf16[12,3072]{1,0:T(8,128)(2,1)S(1)} collective-permute-done((bf16[12,3072]{1,0:T(8,128)(2,1)S(1)}, bf16[12,3072]{1,0:T(8,128)(2,1)S(1)}, u32[]{:S(2)}, u32[]{:S(2)}) %collective-permute-start.15) | collective-permute-done | bytes 73760
  302.7 10.4 %collective-permute-start.8 = (bf16[16,3072]{1,0:T(8,128)(2,1)S(1)}, bf16[16,3072]{1,0:T(8,128)(2,1)S(1)}, u32[]{:S(2)}, u32[]{:S(2)}) collective-permute-start(bf16[16,3072]{1,0:T(8,128)(2,1)S(1)} %get-tuple-element.11), channel_id=1, source_target_pairs={{0,1},{1,2},{2,3},{3,4},{4,5},{5,6},{6,7},{7,8},{8,9},{9,10},{10,1... | collective-permute-start | bytes 294920
  317.6 20.6 %concatenate.1 = bf16[140,3072]{1,0:T(8,128)(2,1)} concatenate(bf16[12,3072]{1,0:T(8,128)(2,1)} %copy-done.15, bf16[16,3072]{1,0:T(8,128)(2,1)} %copy-done.18, bf16[16,3072]{1,0:T(8,128)(2,1)} %copy-done.17, bf16[16,3072]{1,0:T(8,128)(2,1)} %copy-done.16, bf16[16,3072]{1,0:T(8,128)(2,1)} %copy-done.14, bf16[16,3072]{1,0:T(8,128)(2,1)S(1)} %collective-permute-done.10, ...), dimensions={0} | concatenate | bytes 1720320
  341.3 16.4 %all-to-all-start.4 = ((bf16[32,12,3072]{2,1,0:T(8,128)(2,1)}), bf16[32,12,3072]{2,1,0:T(8,128)(2,1)}, u32[]{:S(2)}, u32[]{:S(2)}) async-start(bf16[32,12,3072]{2,1,0:T(8,128)(2,1)} %stack.11), calls=%async_computation.4 | async-start | bytes 6291456 | tf_op jit(solution)/shard_map/all_to_all | solution.py:9
  359.8 72.1 %all-to-all-done.4 = bf16[32,12,3072]{2,1,0:T(8,128)(2,1)} async-done(((bf16[32,12,3072]{2,1,0:T(8,128)(2,1)}), bf16[32,12,3072]{2,1,0:T(8,128)(2,1)}, u32[]{:S(2)}, u32[]{:S(2)}) %all-to-all-start.4) | async-done | bytes 2359328 | tf_op jit(solution)/shard_map/all_to_all | solution.py:9
  431.8 5.9 %all-to-all-start.2 = ((bf16[8,48,3072]{2,1,0:T(8,128)(2,1)}), bf16[8,48,3072]{2,1,0:T(8,128)(2,1)S(1)}, u32[]{:S(2)}, u32[]{:S(2)}) async-start(bf16[8,48,3072]{2,1,0:T(8,128)(2,1)} %reshape_reshape.6), calls=%async_computation.2 | async-start | bytes 4718592 | tf_op jit(solution)/shard_map/all_to_all | solution.py:48
  437.8 4.2 reshape_reshape.7
  442.0 28.2 %all-to-all-done.2 = bf16[8,48,3072]{2,1,0:T(8,128)(2,1)S(1)} async-done(((bf16[8,48,3072]{2,1,0:T(8,128)(2,1)}), bf16[8,48,3072]{2,1,0:T(8,128)(2,1)S(1)}, u32[]{:S(2)}, u32[]{:S(2)}) %all-to-all-start.2) | async-done | bytes 2359328 | tf_op jit(solution)/shard_map/all_to_all | solution.py:48
  470.3 5.4 %all-to-all-start.5 = ((bf16[8,48,3072]{2,1,0:T(8,128)(2,1)}), bf16[8,48,3072]{2,1,0:T(8,128)(2,1)}, u32[]{:S(2)}, u32[]{:S(2)}) async-start(bf16[8,48,3072]{2,1,0:T(8,128)(2,1)} %reshape_reshape.7), calls=%async_computation.5 | async-start | bytes 4718592 | tf_op jit(solution)/shard_map/all_to_all | solution.py:48
  489.1 13.5 %all-to-all-done.5 = bf16[8,48,3072]{2,1,0:T(8,128)(2,1)} async-done(((bf16[8,48,3072]{2,1,0:T(8,128)(2,1)}), bf16[8,48,3072]{2,1,0:T(8,128)(2,1)}, u32[]{:S(2)}, u32[]{:S(2)}) %all-to-all-start.5) | async-done | bytes 2359328 | tf_op jit(solution)/shard_map/all_to_all | solution.py:48
  (109 shorter events, 74.9 us)
Async XLA Ops:
  0.6 76.2 %copy-start = (bf16[1,256,3072]{2,1,0:T(8,128)(2,1)S(1)}, bf16[1,256,3072]{2,1,0:T(8,128)(2,1)}, u32[]{:S(2)}) copy-start(bf16[1,256,3072]{2,1,0:T(8,128)(2,1)} %param.13) | copy-start | bytes 4718596
  7.0 35.5 %all-to-all-start = ((bf16[8,48,3072]{2,1,0:T(8,128)(2,1)}), bf16[8,48,3072]{2,1,0:T(8,128)(2,1)}, u32[]{:S(2)}, u32[]{:S(2)}) async-start(bf16[8,48,3072]{2,1,0:T(8,128)(2,1)} %bitcast.78), calls=%async_computation | async-start | bytes 4718592 | tf_op jit(solution)/shard_map/all_to_all | solution.py:36
  42.6 34.2 %all-to-all-start.3 = ((bf16[8,48,3072]{2,1,0:T(8,128)(2,1)}), bf16[8,48,3072]{2,1,0:T(8,128)(2,1)}, u32[]{:S(2)}, u32[]{:S(2)}) async-start(bf16[8,48,3072]{2,1,0:T(8,128)(2,1)} %bitcast.79), calls=%async_computation.3 | async-start | bytes 4718592 | tf_op jit(solution)/shard_map/all_to_all | solution.py:36
  84.8 111.4 %copy-start.21 = (u32[256]{0:T(256)S(1)}, u32[256]{0:T(256)}, u32[]{:S(2)}) copy-start(u32[256]{0:T(256)} %constant.17) | copy-start | bytes 3076
  170.9 17.8 %collective-permute-start = (bf16[16,3072]{1,0:T(8,128)(2,1)S(1)}, bf16[16,3072]{1,0:T(8,128)(2,1)S(1)}, u32[]{:S(2)}, u32[]{:S(2)}) collective-permute-start(bf16[16,3072]{1,0:T(8,128)(2,1)S(1)} %get-tuple-element.10), channel_id=1, source_target_pairs={{0,1},{1,2},{2,3},{3,4},{4,5},{5,6},{6,7},{7,8},{8,9},{9,10},{10,1... | collective-permute-start | bytes 294920
  172.2 19.3 %collective-permute-start.1 = (bf16[16,3072]{1,0:T(8,128)(2,1)S(1)}, bf16[16,3072]{1,0:T(8,128)(2,1)S(1)}, u32[]{:S(2)}, u32[]{:S(2)}) collective-permute-start(bf16[16,3072]{1,0:T(8,128)(2,1)S(1)} %get-tuple-element.10), channel_id=1, source_target_pairs={{0,2},{1,3},{2,4},{3,5},{4,6},{5,7},{6,8},{7,9},{8,10},{9,11},{10,... | collective-permute-start | bytes 294920
  173.5 13.5 %collective-permute-start.7 = (bf16[12,3072]{1,0:T(8,128)(2,1)S(1)}, bf16[12,3072]{1,0:T(8,128)(2,1)S(1)}, u32[]{:S(2)}, u32[]{:S(2)}) collective-permute-start(bf16[12,3072]{1,0:T(8,128)(2,1)S(1)} %slice.35), channel_id=1, source_target_pairs={{0,8},{1,9},{2,10},{3,11},{4,12},{5,13},{6,14},{7,15},{8,16},{9,17... | collective-permute-start | bytes 221192
  174.8 22.6 %collective-permute-start.2 = (bf16[16,3072]{1,0:T(8,128)(2,1)S(1)}, bf16[16,3072]{1,0:T(8,128)(2,1)S(1)}, u32[]{:S(2)}, u32[]{:S(2)}) collective-permute-start(bf16[16,3072]{1,0:T(8,128)(2,1)S(1)} %get-tuple-element.10), channel_id=1, source_target_pairs={{0,3},{1,4},{2,5},{3,6},{4,7},{5,8},{6,9},{7,10},{8,11},{9,12},{10... | collective-permute-start | bytes 294920
  176.1 21.3 %collective-permute-start.3 = (bf16[16,3072]{1,0:T(8,128)(2,1)S(1)}, bf16[16,3072]{1,0:T(8,128)(2,1)S(1)}, u32[]{:S(2)}, u32[]{:S(2)}) collective-permute-start(bf16[16,3072]{1,0:T(8,128)(2,1)S(1)} %get-tuple-element.10), channel_id=1, source_target_pairs={{0,4},{1,5},{2,6},{3,7},{4,8},{5,9},{6,10},{7,11},{8,12},{9,13},{1... | collective-permute-start | bytes 294920
  187.0 10.4 %collective-permute-start.4 = (bf16[16,3072]{1,0:T(8,128)(2,1)S(1)}, bf16[16,3072]{1,0:T(8,128)(2,1)S(1)}, u32[]{:S(2)}, u32[]{:S(2)}) collective-permute-start(bf16[16,3072]{1,0:T(8,128)(2,1)S(1)} %get-tuple-element.10), channel_id=1, source_target_pairs={{0,5},{1,6},{2,7},{3,8},{4,9},{5,10},{6,11},{7,12},{8,13},{9,14},{... | collective-permute-start | bytes 294920
  188.7 13.9 %collective-permute-start.5 = (bf16[16,3072]{1,0:T(8,128)(2,1)S(1)}, bf16[16,3072]{1,0:T(8,128)(2,1)S(1)}, u32[]{:S(2)}, u32[]{:S(2)}) collective-permute-start(bf16[16,3072]{1,0:T(8,128)(2,1)S(1)} %get-tuple-element.10), channel_id=1, source_target_pairs={{0,6},{1,7},{2,8},{3,9},{4,10},{5,11},{6,12},{7,13},{8,14},{9,15},... | collective-permute-start | bytes 294920
  191.5 16.1 %collective-permute-start.6 = (bf16[16,3072]{1,0:T(8,128)(2,1)S(1)}, bf16[16,3072]{1,0:T(8,128)(2,1)S(1)}, u32[]{:S(2)}, u32[]{:S(2)}) collective-permute-start(bf16[16,3072]{1,0:T(8,128)(2,1)S(1)} %get-tuple-element.10), channel_id=1, source_target_pairs={{0,7},{1,8},{2,9},{3,10},{4,11},{5,12},{6,13},{7,14},{8,15},{9,16}... | collective-permute-start | bytes 294920
  211.7 127.4 %all-to-all-start.1 = ((bf16[32,12,3072]{2,1,0:T(8,128)(2,1)}), bf16[32,12,3072]{2,1,0:T(8,128)(2,1)S(1)}, u32[]{:S(2)}, u32[]{:S(2)}) async-start(bf16[32,12,3072]{2,1,0:T(8,128)(2,1)} %stack.10), calls=%async_computation.1 | async-start | bytes 6291456 | tf_op jit(solution)/shard_map/all_to_all | solution.py:9
  220.2 82.5 %collective-permute-start.10 = (bf16[16,3072]{1,0:T(8,128)(2,1)S(1)}, bf16[16,3072]{1,0:T(8,128)(2,1)S(1)}, u32[]{:S(2)}, u32[]{:S(2)}) collective-permute-start(bf16[16,3072]{1,0:T(8,128)(2,1)S(1)} %get-tuple-element.11), channel_id=1, source_target_pairs={{0,3},{1,4},{2,5},{3,6},{4,7},{5,8},{6,9},{7,10},{8,11},{9,12},{10... | collective-permute-start | bytes 294920
  223.6 89.5 %collective-permute-start.11 = (bf16[16,3072]{1,0:T(8,128)(2,1)S(1)}, bf16[16,3072]{1,0:T(8,128)(2,1)S(1)}, u32[]{:S(2)}, u32[]{:S(2)}) collective-permute-start(bf16[16,3072]{1,0:T(8,128)(2,1)S(1)} %get-tuple-element.11), channel_id=1, source_target_pairs={{0,4},{1,5},{2,6},{3,7},{4,8},{5,9},{6,10},{7,11},{8,12},{9,13},{1... | collective-permute-start | bytes 294920
  227.9 73.5 %collective-permute-start.15 = (bf16[12,3072]{1,0:T(8,128)(2,1)S(1)}, bf16[12,3072]{1,0:T(8,128)(2,1)S(1)}, u32[]{:S(2)}, u32[]{:S(2)}) collective-permute-start(bf16[12,3072]{1,0:T(8,128)(2,1)S(1)} %slice.36), channel_id=1, source_target_pairs={{0,8},{1,9},{2,10},{3,11},{4,12},{5,13},{6,14},{7,15},{8,16},{9,17... | collective-permute-start | bytes 221192
  232.5 82.6 %collective-permute-start.12 = (bf16[16,3072]{1,0:T(8,128)(2,1)S(1)}, bf16[16,3072]{1,0:T(8,128)(2,1)S(1)}, u32[]{:S(2)}, u32[]{:S(2)}) collective-permute-start(bf16[16,3072]{1,0:T(8,128)(2,1)S(1)} %get-tuple-element.11), channel_id=1, source_target_pairs={{0,5},{1,6},{2,7},{3,8},{4,9},{5,10},{6,11},{7,12},{8,13},{9,14},{... | collective-permute-start | bytes 294920
  238.6 76.5 %collective-permute-start.13 = (bf16[16,3072]{1,0:T(8,128)(2,1)S(1)}, bf16[16,3072]{1,0:T(8,128)(2,1)S(1)}, u32[]{:S(2)}, u32[]{:S(2)}) collective-permute-start(bf16[16,3072]{1,0:T(8,128)(2,1)S(1)} %get-tuple-element.11), channel_id=1, source_target_pairs={{0,6},{1,7},{2,8},{3,9},{4,10},{5,11},{6,12},{7,13},{8,14},{9,15},... | collective-permute-start | bytes 294920
  301.4 13.9 %collective-permute-start.14 = (bf16[16,3072]{1,0:T(8,128)(2,1)S(1)}, bf16[16,3072]{1,0:T(8,128)(2,1)S(1)}, u32[]{:S(2)}, u32[]{:S(2)}) collective-permute-start(bf16[16,3072]{1,0:T(8,128)(2,1)S(1)} %get-tuple-element.11), channel_id=1, source_target_pairs={{0,7},{1,8},{2,9},{3,10},{4,11},{5,12},{6,13},{7,14},{8,15},{9,16}... | collective-permute-start | bytes 294920
  302.7 12.6 %collective-permute-start.8 = (bf16[16,3072]{1,0:T(8,128)(2,1)S(1)}, bf16[16,3072]{1,0:T(8,128)(2,1)S(1)}, u32[]{:S(2)}, u32[]{:S(2)}) collective-permute-start(bf16[16,3072]{1,0:T(8,128)(2,1)S(1)} %get-tuple-element.11), channel_id=1, source_target_pairs={{0,1},{1,2},{2,3},{3,4},{4,5},{5,6},{6,7},{7,8},{8,9},{9,10},{10,1... | collective-permute-start | bytes 294920
  313.1 4.5 collective-permute-start.9
  341.3 90.6 %all-to-all-start.4 = ((bf16[32,12,3072]{2,1,0:T(8,128)(2,1)}), bf16[32,12,3072]{2,1,0:T(8,128)(2,1)}, u32[]{:S(2)}, u32[]{:S(2)}) async-start(bf16[32,12,3072]{2,1,0:T(8,128)(2,1)} %stack.11), calls=%async_computation.4 | async-start | bytes 6291456 | tf_op jit(solution)/shard_map/all_to_all | solution.py:9
  431.8 38.4 %all-to-all-start.2 = ((bf16[8,48,3072]{2,1,0:T(8,128)(2,1)}), bf16[8,48,3072]{2,1,0:T(8,128)(2,1)S(1)}, u32[]{:S(2)}, u32[]{:S(2)}) async-start(bf16[8,48,3072]{2,1,0:T(8,128)(2,1)} %reshape_reshape.6), calls=%async_computation.2 | async-start | bytes 4718592 | tf_op jit(solution)/shard_map/all_to_all | solution.py:48
  470.3 32.3 %all-to-all-start.5 = ((bf16[8,48,3072]{2,1,0:T(8,128)(2,1)}), bf16[8,48,3072]{2,1,0:T(8,128)(2,1)}, u32[]{:S(2)}, u32[]{:S(2)}) async-start(bf16[8,48,3072]{2,1,0:T(8,128)(2,1)} %reshape_reshape.7), calls=%async_computation.5 | async-start | bytes 4718592 | tf_op jit(solution)/shard_map/all_to_all | solution.py:48
  (20 other events, 81.4 us)
